TPU v7x, 256 devices: a whole 4x4x8 slice. The times are simulated.
256 devices in a mesh: row: 32 (over z, y_lo, core), col: 8 (over y_hi, x).
Axes of the slice: x: 4, y: 4 (y_hi: 2, y_lo: 2; y = y_hi * 2 + y_lo), z: 8, core: 2. Of those that a mesh axis runs over, the one named last changes fastest.
Arguments:
- coupling: bfloat16 [16384, 4096], P('row', 'col'), may hold values from 0.19921875 to 5
- source_dist: bfloat16 [16384, 16384], P('row'), may hold values from -0.013531647 to 0.013531647, as said below
- target_dist: bfloat16 [4096, 4096], P('row', 'col'), may hold values from -0.09375 to 0.09375
- source_feat: bfloat16 [16384, 256], P('row'), may hold values from -3.5 to 3.5
- target_feat: bfloat16 [4096, 256], P('col'), may hold values from -3.5 to 3.5
- source_type: int32 [16384], P('row'), may hold values from 0 to 15
- target_type: int32 [4096], P('col'), may hold values from 0 to 15
- row_weight: float32 [16384], P('row'), may hold values from 0.5 to 10
- col_weight: float32 [4096], P('col'), may hold values from 0.5 to 2
Outputs:
- coupling_next: bfloat16 [16384, 4096], P('row', 'col')
- barycentre: bfloat16 [16384, 256], P(('row', 'col'))
Inputs may be any that keep to these rules, and one draw needn't show every extreme that they name: `source_dist`: symmetric.
All inputs are finite; a program needn't handle non-finite values.
Results may differ from a plain program's by a relative error of at most 0.02.
Values may be sent and summed in bfloat16 or wider, within the bound.
A program may use at most 128 MiB of HBM per device.

v0:
```python
import math
import jax
import jax.numpy as jnp
from jax import lax
from jax.sharding import PartitionSpec as P

coupling_weight = 0.5
feature_weight = 2.5
mismatch_cost = 1.0


def from_everyone(value, axis):
    copies = jnp.broadcast_to(value, (lax.axis_size(axis), *value.shape))
    return lax.all_to_all(copies, axis, split_axis=0, concat_axis=0, tiled=True)


def all_in_one(value, axis):
    leaves = jax.tree.leaves(value)
    turns = sorted(range(len(leaves)), key=lambda k: -leaves[k].size)
    width = (1, *leaves[turns[0]].shape)[-1]
    lines = [
        jnp.pad(leaves[k].reshape(-1), (0, -leaves[k].size % width)).reshape(-1, width)
        for k in turns
    ]
    both, at, found = (from_everyone(jnp.concatenate(lines), axis), 0, {})
    for k, line in zip(turns, lines):
        share = both[:, at : at + len(line)].reshape(len(both), -1)
        found[k] = share[:, : leaves[k].size].reshape(-1, *leaves[k].shape)
        at += len(line)
    numbers = iter(range(len(leaves)))
    return jax.tree.map(lambda _: found[next(numbers)], value)


def combined_pairwise(pieces, combine):
    while len(jax.tree.leaves(pieces)[0]) > 1:
        pieces = jax.vmap(combine)(
            *(jax.tree.map(lambda part: part[side::2], pieces) for side in (0, 1))
        )
    return jax.tree.map(lambda part: part[0], pieces)


def combined_all(value, axis, combine):
    pieces = all_in_one(value, axis)
    return combined_pairwise(pieces, combine)


def gathered_by_type(value, axis):
    leaves, found = (jax.tree.leaves(value), {})
    for first, a in enumerate(leaves):
        if first not in found:
            alike = [k for k, b in enumerate(leaves) if b.dtype == a.dtype]
            got = (
                all_in_one([leaves[k] for k in alike], axis)
                if len(alike) > 1
                else [from_everyone(a, axis)]
            )
            for k, b in zip(alike, got):
                found[k] = b
    numbers = iter(range(len(leaves)))
    return jax.tree.map(lambda _: found[next(numbers)], value)


def combined_all_2(value, axis, combine):
    pieces = gathered_by_type(value, axis)
    return combined_pairwise(pieces, combine)


def split_up(value, dim, length):
    lengths = value.shape
    pieces = value.reshape(*lengths[:dim], length, lengths[dim] // length, *lengths[dim + 1 :])
    return jnp.moveaxis(pieces, dim, 0)


def summed_on_arrival(value, axis, dim):
    length = lax.axis_size(axis)
    pieces = lax.all_to_all(split_up(value, dim, length), axis, 0, 0, tiled=True)
    return jnp.sum(pieces.astype(jnp.float32), axis=0)


def combine_stats(earlier, later):
    highest = jnp.maximum(earlier[0], later[0])
    return (
        highest,
        earlier[1] * jnp.exp(earlier[0] - highest) + later[1] * jnp.exp(later[0] - highest),
    )


def shards(
    coupling,
    source_dist,
    target_dist,
    source_feat,
    target_feat,
    source_type,
    target_type,
    row_weight,
    col_weight,
):
    row_count, col_count = coupling.shape
    feat_width = source_feat.shape[1]
    total_rows = row_count * lax.axis_size("row")
    total_cols = col_count * lax.axis_size("col")
    target_block = lax.all_gather(target_dist, "row", axis=0, tiled=True)
    first = jnp.dot(
        source_dist,
        lax.all_gather(coupling, "row", axis=0, tiled=True),
        preferred_element_type=jnp.float32,
    )
    first_whole = lax.all_gather(first.astype(jnp.bfloat16), "col", axis=1, tiled=True)
    second = jnp.dot(first_whole, target_block, preferred_element_type=jnp.float32)
    affinity = lax.dot_general(
        source_feat, target_feat, (((1,), (1,)), ((), ())), preferred_element_type=jnp.float32
    )
    mismatch = (source_type[:, None] != target_type[None, :]).astype(jnp.float32)
    score = (
        jnp.log(coupling.astype(jnp.float32))
        + coupling_weight * second
        + feature_weight / math.sqrt(feat_width) * affinity
        - mismatch_cost * mismatch
    )
    local_top = jnp.max(score, axis=1)
    local_sum = jnp.sum(jnp.exp(score - local_top[:, None]), axis=1)
    row_top, row_sum = combined_all((local_top, local_sum), "col", combine_stats)
    row_lse = row_top + jnp.log(row_sum)
    first_log = score - row_lse[:, None] + jnp.log(row_weight)[:, None] + math.log(total_cols)
    local_col_top = jnp.max(first_log, axis=0)
    local_col_sum = jnp.sum(jnp.exp(first_log - local_col_top[None, :]), axis=0)
    col_top, col_sum = combined_all_2((local_col_top, local_col_sum), "row", combine_stats)
    col_lse = col_top + jnp.log(col_sum)
    next_float = jnp.exp(
        first_log - col_lse[None, :] + jnp.log(col_weight)[None, :] + math.log(total_rows)
    )
    coupling_next = next_float.astype(jnp.bfloat16)
    numer = jnp.dot(coupling_next, target_feat, preferred_element_type=jnp.float32)
    mass = jnp.sum(next_float, axis=1, keepdims=True)
    numer_home, mass_home = (
        summed_on_arrival(numer.astype(jnp.bfloat16), "col", 0),
        summed_on_arrival(mass.astype(jnp.bfloat16), "col", 0),
    )
    return (coupling_next, (numer_home / mass_home).astype(jnp.bfloat16))


def solution(mesh):
    in_specs = (
        P("row", "col"),
        P("row", None),
        P("row", "col"),
        P("row", None),
        P("col", None),
        P("row"),
        P("col"),
        P("row"),
        P("col"),
    )
    out_specs = (P("row", "col"), P(("row", "col"), None))
    return jax.shard_map(shards, mesh=mesh, in_specs=in_specs, out_specs=out_specs, check_vma=False)
```

profile of v0, /device:TPU:8, one launch (start us, length us, event | category | flops | bytes accessed | tf_op | source)
XLA Modules:
  0.0 336.4 jit_solution(761586258189664936)
XLA Ops:
  7.2 0.0 copy-start
  7.2 0.0 all-gather.4.cloned.1.call-start
  7.2 0.7 all-gather.4.cloned.1.call-update
  7.9 0.0 all-gather.8.cloned.1.call-start
  8.0 0.7 all-gather.8.cloned.1.call-update
  8.7 0.0 copy-start.1
  8.7 0.0 all-gather.6.cloned.1.call-start
  8.7 103.6 %all-gather.4.cloned.1.call-done = bf16[16384,512]{1,0:T(8,128)(2,1)} async-done(((bf16[512,512]{1,0:T(8,128)(2,1)}), bf16[16384,512]{1,0:T(8,128)(2,1)}) %all-gather.4.cloned.1.call-update) | async-done | bytes 16777232 | tf_op jit(solution)/shard_map/all_gather | solution.py:106
  112.4 17.9 %convolution_convert_fusion = bf16[512,512]{1,0:T(8,128)(2,1)} fusion(bf16[512,16384]{1,0:T(8,128)(2,1)} %param.10, bf16[16384,512]{1,0:T(8,128)(2,1)} %all-gather.4.cloned.1.call-done), kind=kOutput, calls=%fused_computation.5 | convolution fusion | flops 8590196736 | bytes 34078720 | tf_op jit(solution)/shard_map/dot_general | solution.py:104
  130.2 0.0 copy-start.2
  130.2 0.0 copy-start.5
  130.2 0.0 copy-start.6
  130.2 0.0 copy-start.3
  130.2 0.0 copy-start.4
  130.3 0.0 all-gather.6.cloned.1.call-update
  130.3 0.0 copy-done.1
  130.3 0.2 copy.19
  130.5 50.3 %all-gather.8.cloned.1.call-done = bf16[4096,512]{1,0:T(8,128)(2,1)} async-done(((bf16[128,512]{1,0:T(8,128)(2,1)}), bf16[4096,512]{1,0:T(8,128)(2,1)}) %all-gather.8.cloned.1.call-update) | async-done | bytes 4194320 | tf_op jit(solution)/shard_map/all_gather | solution.py:103
  180.8 84.8 %all-gather.6.cloned.1.call-done = bf16[512,4096]{1,0:T(8,128)(2,1)} async-done(((bf16[512,512]{1,0:T(8,128)(2,1)}), bf16[512,4096]{1,0:T(8,128)(2,1)}) %all-gather.6.cloned.1.call-update) | async-done | bytes 4194320 | tf_op jit(solution)/shard_map/all_gather | solution.py:109
  265.6 5.9 %fusion.2 = f32[512,512]{0,1:T(8,128)S(1)} fusion(bf16[512,4096]{1,0:T(8,128)(2,1)} %all-gather.6.cloned.1.call-done, bf16[4096,512]{1,0:T(8,128)(2,1)} %all-gather.8.cloned.1.call-done, bf16[512,512]{0,1:T(8,128)(2,1)S(1)} %copy.19), kind=kOutput, calls=%fused_computation.4 | convolution fusion | flops 2148270080 | bytes 9961472 | tf_op jit(solution)/shard_map/dot_general | solution.py:110
  271.5 0.0 copy-done
  271.5 0.0 copy-done.2
  271.5 0.0 copy-done.5
  271.5 0.0 copy-done.6
  271.5 0.4 fusion.12
  271.9 0.2 exponential_reduce_fusion.1
  272.1 0.6 broadcast_in_dim.4
  272.8 4.5 %all-to-all-start = ((f32[8,2,512]{2,1,0:T(2,128)}), f32[8,2,512]{2,1,0:T(2,128)S(1)}, u32[]{:S(2)}, u32[]{:S(2)}) async-start(f32[8,2,512]{2,1,0:T(2,128)} %broadcast_in_dim.4), calls=%async_computation | async-start | bytes 65536 | tf_op jit(solution)/shard_map/all_to_all | solution.py:14
  277.3 0.0 copy-done.3
  277.3 7.7 %all-to-all-done = f32[8,2,512]{2,1,0:T(2,128)S(1)} async-done(((f32[8,2,512]{2,1,0:T(2,128)}), f32[8,2,512]{2,1,0:T(2,128)S(1)}, u32[]{:S(2)}, u32[]{:S(2)}) %all-to-all-start) | async-done | bytes 32800 | tf_op jit(solution)/shard_map/all_to_all | solution.py:14
  285.3 0.2 fusion.5
  285.6 0.4 exponential_reduce_fusion
  285.9 0.7 broadcast_in_dim.5
  286.6 8.6 %all-to-all-start.1 = ((f32[32,2,512]{2,1,0:T(2,128)}), f32[32,2,512]{2,1,0:T(2,128)S(1)}, u32[]{:S(2)}, u32[]{:S(2)}) async-start(f32[32,2,512]{2,1,0:T(2,128)} %broadcast_in_dim.5), calls=%async_computation.1 | async-start | bytes 262144 | tf_op jit(solution)/shard_map/all_to_all | solution.py:14
  295.3 0.0 copy-done.4
  295.3 9.2 %all-to-all-done.1 = f32[32,2,512]{2,1,0:T(2,128)S(1)} async-done(((f32[32,2,512]{2,1,0:T(2,128)}), f32[32,2,512]{2,1,0:T(2,128)S(1)}, u32[]{:S(2)}, u32[]{:S(2)}) %all-to-all-start.1) | async-done | bytes 131104 | tf_op jit(solution)/shard_map/all_to_all | solution.py:14
  304.5 0.1 fusion.10
  305.1 0.4 fusion.3
  305.5 0.7 convert_element_type.49
  306.2 3.3 all-to-all-start.3
  309.5 1.1 convolution_convert_fusion.1
  310.5 6.5 %all-to-all-done.3 = bf16[8,64,1]{1,2,0:T(2,128)(2,1)S(1)} async-done(((bf16[8,64,1]{1,2,0:T(2,128)(2,1)}), bf16[8,64,1]{1,2,0:T(2,128)(2,1)S(1)}, u32[]{:S(2)}, u32[]{:S(2)}) %all-to-all-start.3) | async-done | bytes 1056 | tf_op jit(solution)/shard_map/all_to_all | solution.py:76
  317.0 3.4 %all-to-all-start.2 = ((bf16[8,64,256]{2,1,0:T(8,128)(2,1)}), bf16[8,64,256]{2,1,0:T(8,128)(2,1)S(1)}, u32[]{:S(2)}, u32[]{:S(2)}) async-start(bf16[8,64,256]{2,1,0:T(8,128)(2,1)} %bitcast.8), calls=%async_computation.2 | async-start | bytes 524288 | tf_op jit(solution)/shard_map/all_to_all | solution.py:76
  320.4 1.0 copy.23
  321.5 7.7 %all-to-all-done.2 = bf16[8,64,256]{2,1,0:T(8,128)(2,1)S(1)} async-done(((bf16[8,64,256]{2,1,0:T(8,128)(2,1)}), bf16[8,64,256]{2,1,0:T(8,128)(2,1)S(1)}, u32[]{:S(2)}, u32[]{:S(2)}) %all-to-all-start.2) | async-done | bytes 262176 | tf_op jit(solution)/shard_map/all_to_all | solution.py:76
  329.2 0.7 divide_convert_fusion
  (42 shorter events, 0.8 us)
Async XLA Ops:
  7.2 264.3 %copy-start = (bf16[512,256]{1,0:T(8,128)(2,1)S(1)}, bf16[512,256]{1,0:T(8,128)(2,1)}, u32[]{:S(2)}) copy-start(bf16[512,256]{1,0:T(8,128)(2,1)} %param.13) | copy-start | bytes 786436
  7.2 105.2 %all-gather.4.cloned.1.call-start = ((), (), s32[]{:S(2)}) async-start(), calls=%async_computation.4 | async-start | bytes 17301504 | tf_op jit(solution)/shard_map/all_gather | solution.py:106
  7.9 172.9 %all-gather.8.cloned.1.call-start = ((), (), s32[]{:S(2)}) async-start(), calls=%async_computation.6 | async-start | bytes 4325376 | tf_op jit(solution)/shard_map/all_gather | solution.py:103
  8.7 121.6 %copy-start.1 = (bf16[512,512]{1,0:T(8,128)(2,1)S(1)}, bf16[512,512]{1,0:T(8,128)(2,1)}, u32[]{:S(2)}) copy-start(bf16[512,512]{1,0:T(8,128)(2,1)} %param.9) | copy-start | bytes 1572868
  8.7 256.9 %all-gather.6.cloned.1.call-start = ((), (), s32[]{:S(2)}) async-start(), calls=%async_computation.5 | async-start | bytes 4718592 | tf_op jit(solution)/shard_map/all_gather | solution.py:109
  130.2 141.3 %copy-start.2 = (bf16[512,256]{1,0:T(8,128)(2,1)S(1)}, bf16[512,256]{1,0:T(8,128)(2,1)}, u32[]{:S(2)}) copy-start(bf16[512,256]{1,0:T(8,128)(2,1)} %param.12) | copy-start | bytes 786436
  130.2 141.3 %copy-start.5 = (s32[512]{0:T(512)S(1)}, s32[512]{0:T(512)}, u32[]{:S(2)}) copy-start(s32[512]{0:T(512)} %param.15) | copy-start | bytes 6148
  130.2 141.3 %copy-start.6 = (s32[512]{0:T(512)S(1)}, s32[512]{0:T(512)}, u32[]{:S(2)}) copy-start(s32[512]{0:T(512)} %param.14) | copy-start | bytes 6148
  130.2 147.0 %copy-start.3 = (f32[512]{0:T(512)S(1)}, f32[512]{0:T(512)}, u32[]{:S(2)}) copy-start(f32[512]{0:T(512)} %param.16) | copy-start | bytes 6148
  130.2 165.0 %copy-start.4 = (f32[512]{0:T(512)S(1)}, f32[512]{0:T(512)}, u32[]{:S(2)}) copy-start(f32[512]{0:T(512)} %param.17) | copy-start | bytes 6148
  272.8 12.3 %all-to-all-start = ((f32[8,2,512]{2,1,0:T(2,128)}), f32[8,2,512]{2,1,0:T(2,128)S(1)}, u32[]{:S(2)}, u32[]{:S(2)}) async-start(f32[8,2,512]{2,1,0:T(2,128)} %broadcast_in_dim.4), calls=%async_computation | async-start | bytes 65536 | tf_op jit(solution)/shard_map/all_to_all | solution.py:14
  286.6 17.9 %all-to-all-start.1 = ((f32[32,2,512]{2,1,0:T(2,128)}), f32[32,2,512]{2,1,0:T(2,128)S(1)}, u32[]{:S(2)}, u32[]{:S(2)}) async-start(f32[32,2,512]{2,1,0:T(2,128)} %broadcast_in_dim.5), calls=%async_computation.1 | async-start | bytes 262144 | tf_op jit(solution)/shard_map/all_to_all | solution.py:14
  306.2 10.9 %all-to-all-start.3 = ((bf16[8,64,1]{1,2,0:T(2,128)(2,1)}), bf16[8,64,1]{1,2,0:T(2,128)(2,1)S(1)}, u32[]{:S(2)}, u32[]{:S(2)}) async-start(bf16[8,64,1]{1,2,0:T(2,128)(2,1)} %convert_element_type.49), calls=%async_computation.3 | async-start | bytes 8192 | tf_op jit(solution)/shard_map/all_to_all | solution.py:76
  317.0 12.1 %all-to-all-start.2 = ((bf16[8,64,256]{2,1,0:T(8,128)(2,1)}), bf16[8,64,256]{2,1,0:T(8,128)(2,1)S(1)}, u32[]{:S(2)}, u32[]{:S(2)}) async-start(bf16[8,64,256]{2,1,0:T(8,128)(2,1)} %bitcast.8), calls=%async_computation.2 | async-start | bytes 524288 | tf_op jit(solution)/shard_map/all_to_all | solution.py:76
Sparse Core Ops, SparseCore 0:
  9.8 102.4 all-gather.3
  114.2 66.5 all-gather.7
  183.9 81.6 all-gather.5
where the time goes:
time: 337 us; the launch traced here: 336 us
  waiting for transfers between devices  271 us (80%)
  matrix products  25.2 us (7%)
  starting transfers between devices  20 us (6%)
  between operations  14 us (4%)
  local copies, waits for them, and re-layouts  3.93 us (1%)
    all_gather x1, waiting for transfers between devices, shards(): lax.all_gather(coupling, 'row', axis=0, tiled=True)  104 us
    all_gather x1, waiting for transfers between devices, shards(): lax.all_gather(first.astype(jnp.bfloat16), 'col', axis=1, tiled=True)  84.8 us
    all_gather x1, waiting for transfers between devices, shards(): target_block = lax.all_gather(target_dist, 'row', axis=0, tiled=True)  50.3 us
    dot_general x1, matrix products, shards(): jnp.dot(source_dist, lax.all_gather(coupling, 'row', axis=0, tiled=True),...  17.9 us
    all_to_all x2, waiting for transfers between devices, from_everyone(): return lax.all_to_all(copies, axis, split_axis=0, concat_axis=0, tiled=True)  17 us
    all_to_all x2, waiting for transfers between devices, summed_on_arrival(): lax.all_to_all(split_up(value, dim, length), axis, 0, 0, tiled=True)  14.2 us
    all_to_all x2, starting transfers between devices, from_everyone(): return lax.all_to_all(copies, axis, split_axis=0, concat_axis=0, tiled=True)  13.2 us
  transfers between devices with their start and end apart: 7, of which 7 were waited for; matrix products, arithmetic and copies ran while one was open for 6% of the time, Pallas kernels for 0%

commit v1 on v0

--- a/solution.py
+++ b/solution.py
@@ -106,7 +106,10 @@
         lax.all_gather(coupling, "row", axis=0, tiled=True),
         preferred_element_type=jnp.float32,
     )
-    first_whole = lax.all_gather(first.astype(jnp.bfloat16), "col", axis=1, tiled=True)
+    first_whole = jnp.concatenate(
+        lax.all_to_all(jnp.stack([first.astype(jnp.bfloat16)] * lax.axis_size("col")), "col", 0, 0),
+        axis=1,
+    )
     second = jnp.dot(first_whole, target_block, preferred_element_type=jnp.float32)
     affinity = lax.dot_general(
         source_feat, target_feat, (((1,), (1,)), ((), ())), preferred_element_type=jnp.float32

time: 337 us -> 284 us (0.84)
  waiting for transfers between devices: 271 us -> 211 us
  starting transfers between devices: 20 us -> 25.1 us
    all_gather x1 -> x0, waiting for transfers between devices: 84.8 us -> none  [shards(): lax.all_gather(first.astype(jnp.bfloat16), 'col', axis=1, tiled=True)]
    all_gather x1, waiting for transfers between devices: 50.3 us -> 75 us  [shards(): target_block = lax.all_gather(target_dist, 'row', axis=0, tiled=True)]
    all_to_all x0 -> x1, starting transfers between devices: none -> 5.94 us  [shards(): lax.all_to_all(jnp.stack([first.astype(jnp.bfloat16)] * lax.axis_size('co...]
  transfers between devices with their start and end apart: 7 -> 7, of which waited for: 7 -> 6; matrix products, arithmetic and copies ran while one was open for 6% -> 8% of each run, Pallas kernels for 0% -> 0%
where the time goes in v1:
time: 284 us
  waiting for transfers between devices  211 us (74%)
  starting transfers between devices  25.1 us (9%)
  matrix products  24.5 us (9%)
  between operations  14.3 us (5%)
  local copies, waits for them, and re-layouts  6.48 us (2%)
    all_gather x1, waiting for transfers between devices, shards(): lax.all_gather(coupling, 'row', axis=0, tiled=True)  104 us
    all_gather x1, waiting for transfers between devices, shards(): target_block = lax.all_gather(target_dist, 'row', axis=0, tiled=True)  75 us
    dot_general x1, matrix products, shards(): jnp.dot(source_dist, lax.all_gather(coupling, 'row', axis=0, tiled=True),...  17.2 us
    all_to_all x2, waiting for transfers between devices, from_everyone(): return lax.all_to_all(copies, axis, split_axis=0, concat_axis=0, tiled=True)  17 us
    all_to_all x2, waiting for transfers between devices, summed_on_arrival(): lax.all_to_all(split_up(value, dim, length), axis, 0, 0, tiled=True)  14.2 us
    all_to_all x2, starting transfers between devices, from_everyone(): return lax.all_to_all(copies, axis, split_axis=0, concat_axis=0, tiled=True)  12.3 us
    all_to_all x2, starting transfers between devices, summed_on_arrival(): lax.all_to_all(split_up(value, dim, length), axis, 0, 0, tiled=True)  6.72 us
    all_to_all x1, starting transfers between devices, shards(): lax.all_to_all(jnp.stack([first.astype(jnp.bfloat16)] * lax.axis_size('co...  5.94 us
  transfers between devices with their start and end apart: 7, of which 6 were waited for; matrix products, arithmetic and copies ran while one was open for 8% of the time, Pallas kernels for 0%

profile of v1, /device:TPU:8, one launch (start us, length us, event | category | flops | bytes accessed | tf_op | source)
XLA Modules:
  0.0 283.7 jit_solution(8209539310525563156)
XLA Ops:
  7.2 0.0 copy-start
  7.2 0.0 all-gather.3.cloned.1.call-start
  7.2 0.7 all-gather.3.cloned.1.call-update
  7.9 0.0 all-gather.5.cloned.1.call-start
  8.0 0.7 all-gather.5.cloned.1.call-update
  8.7 103.7 %all-gather.3.cloned.1.call-done = bf16[16384,512]{1,0:T(8,128)(2,1)} async-done(((bf16[512,512]{1,0:T(8,128)(2,1)}), bf16[16384,512]{1,0:T(8,128)(2,1)}) %all-gather.3.cloned.1.call-update) | async-done | bytes 16777232 | tf_op jit(solution)/shard_map/all_gather | solution.py:106
  112.4 17.2 %convolution_convert_fusion = bf16[512,512]{1,0:T(8,128)(2,1)S(1)} fusion(bf16[512,16384]{1,0:T(8,128)(2,1)} %param.10, bf16[16384,512]{1,0:T(8,128)(2,1)} %all-gather.3.cloned.1.call-done), kind=kOutput, calls=%fused_computation.5 | convolution fusion | flops 8590196736 | bytes 34078720 | tf_op jit(solution)/shard_map/dot_general | solution.py:104
  129.5 0.2 copy.21
  129.8 2.3 stack.2
  132.1 0.0 copy-start.1
  132.1 5.9 %all-to-all-start = ((bf16[8,512,512]{1,2,0:T(8,128)(2,1)}), bf16[8,512,512]{1,2,0:T(8,128)(2,1)}, u32[]{:S(2)}, u32[]{:S(2)}) async-start(bf16[8,512,512]{1,2,0:T(8,128)(2,1)} %stack.2), calls=%async_computation | async-start | bytes 8388608 | tf_op jit(solution)/shard_map/all_to_all | solution.py:110
  138.0 0.0 copy-done.1
  138.0 0.2 copy.20
  138.3 75.0 %all-gather.5.cloned.1.call-done = bf16[4096,512]{1,0:T(8,128)(2,1)} async-done(((bf16[128,512]{1,0:T(8,128)(2,1)}), bf16[4096,512]{1,0:T(8,128)(2,1)}) %all-gather.5.cloned.1.call-update) | async-done | bytes 4194320 | tf_op jit(solution)/shard_map/all_gather | solution.py:103
  213.3 0.0 all-to-all-done
  213.3 0.0 copy-start.2
  213.3 0.0 copy-start.5
  213.3 0.0 copy-start.6
  213.3 0.0 copy-start.3
  213.3 5.9 %fusion.2 = f32[512,512]{0,1:T(8,128)S(1)} fusion(bf16[512,4096]{0,1:T(8,128)(2,1)} %bitcast.1, bf16[4096,512]{1,0:T(8,128)(2,1)} %all-gather.5.cloned.1.call-done, bf16[512,512]{0,1:T(8,128)(2,1)S(1)} %copy.20), kind=kOutput, calls=%fused_computation.4 | convolution fusion | flops 2148270080 | bytes 9961472 | tf_op jit(solution)/shard_map/dot_general | solution.py:113
  219.2 0.0 copy-done
  219.2 0.0 copy-done.2
  219.2 0.0 copy-done.5
  219.2 0.0 copy-done.6
  219.2 0.0 copy-start.4
  219.2 0.4 fusion.12
  219.6 0.2 exponential_reduce_fusion.1
  219.8 0.6 broadcast_in_dim.4
  220.5 5.9 %all-to-all-start.1 = ((f32[8,2,512]{2,1,0:T(2,128)}), f32[8,2,512]{2,1,0:T(2,128)S(1)}, u32[]{:S(2)}, u32[]{:S(2)}) async-start(f32[8,2,512]{2,1,0:T(2,128)} %broadcast_in_dim.4), calls=%async_computation.1 | async-start | bytes 65536 | tf_op jit(solution)/shard_map/all_to_all | solution.py:14
  226.4 0.0 copy-done.3
  226.4 7.7 %all-to-all-done.1 = f32[8,2,512]{2,1,0:T(2,128)S(1)} async-done(((f32[8,2,512]{2,1,0:T(2,128)}), f32[8,2,512]{2,1,0:T(2,128)S(1)}, u32[]{:S(2)}, u32[]{:S(2)}) %all-to-all-start.1) | async-done | bytes 32800 | tf_op jit(solution)/shard_map/all_to_all | solution.py:14
  234.5 0.2 fusion.5
  234.7 0.4 exponential_reduce_fusion
  235.1 0.7 broadcast_in_dim.5
  235.7 6.4 %all-to-all-start.2 = ((f32[32,2,512]{2,1,0:T(2,128)}), f32[32,2,512]{2,1,0:T(2,128)S(1)}, u32[]{:S(2)}, u32[]{:S(2)}) async-start(f32[32,2,512]{2,1,0:T(2,128)} %broadcast_in_dim.5), calls=%async_computation.2 | async-start | bytes 262144 | tf_op jit(solution)/shard_map/all_to_all | solution.py:14
  242.2 0.0 copy-done.4
  242.2 9.2 %all-to-all-done.2 = f32[32,2,512]{2,1,0:T(2,128)S(1)} async-done(((f32[32,2,512]{2,1,0:T(2,128)}), f32[32,2,512]{2,1,0:T(2,128)S(1)}, u32[]{:S(2)}, u32[]{:S(2)}) %all-to-all-start.2) | async-done | bytes 131104 | tf_op jit(solution)/shard_map/all_to_all | solution.py:14
  251.4 0.1 fusion.10
  252.0 0.4 fusion.3
  252.4 0.7 convert_element_type.49
  253.1 3.3 %all-to-all-start.4 = ((bf16[8,64,1]{1,2,0:T(2,128)(2,1)}), bf16[8,64,1]{1,2,0:T(2,128)(2,1)S(1)}, u32[]{:S(2)}, u32[]{:S(2)}) async-start(bf16[8,64,1]{1,2,0:T(2,128)(2,1)} %convert_element_type.49), calls=%async_computation.4 | async-start | bytes 8192 | tf_op jit(solution)/shard_map/all_to_all | solution.py:76
  256.4 1.0 convolution_convert_fusion.1
  257.4 6.5 %all-to-all-done.4 = bf16[8,64,1]{1,2,0:T(2,128)(2,1)S(1)} async-done(((bf16[8,64,1]{1,2,0:T(2,128)(2,1)}), bf16[8,64,1]{1,2,0:T(2,128)(2,1)S(1)}, u32[]{:S(2)}, u32[]{:S(2)}) %all-to-all-start.4) | async-done | bytes 1056 | tf_op jit(solution)/shard_map/all_to_all | solution.py:76
  263.9 3.4 %all-to-all-start.3 = ((bf16[8,64,256]{2,1,0:T(8,128)(2,1)}), bf16[8,64,256]{2,1,0:T(8,128)(2,1)S(1)}, u32[]{:S(2)}, u32[]{:S(2)}) async-start(bf16[8,64,256]{2,1,0:T(8,128)(2,1)} %bitcast.10), calls=%async_computation.3 | async-start | bytes 524288 | tf_op jit(solution)/shard_map/all_to_all | solution.py:76
  267.4 1.0 copy.25
  268.4 7.7 %all-to-all-done.3 = bf16[8,64,256]{2,1,0:T(8,128)(2,1)S(1)} async-done(((bf16[8,64,256]{2,1,0:T(8,128)(2,1)}), bf16[8,64,256]{2,1,0:T(8,128)(2,1)S(1)}, u32[]{:S(2)}, u32[]{:S(2)}) %all-to-all-start.3) | async-done | bytes 262176 | tf_op jit(solution)/shard_map/all_to_all | solution.py:76
  276.1 0.7 divide_convert_fusion
  (42 shorter events, 0.8 us)
Async XLA Ops:
  7.2 212.0 %copy-start = (bf16[512,256]{1,0:T(8,128)(2,1)S(1)}, bf16[512,256]{1,0:T(8,128)(2,1)}, u32[]{:S(2)}) copy-start(bf16[512,256]{1,0:T(8,128)(2,1)} %param.13) | copy-start | bytes 786436
  7.2 105.2 %all-gather.3.cloned.1.call-start = ((), (), s32[]{:S(2)}) async-start(), calls=%async_computation.5 | async-start | bytes 17301504 | tf_op jit(solution)/shard_map/all_gather | solution.py:106
  7.9 205.3 %all-gather.5.cloned.1.call-start = ((), (), s32[]{:S(2)}) async-start(), calls=%async_computation.6 | async-start | bytes 4325376 | tf_op jit(solution)/shard_map/all_gather | solution.py:103
  132.1 5.9 %copy-start.1 = (bf16[512,512]{1,0:T(8,128)(2,1)S(1)}, bf16[512,512]{1,0:T(8,128)(2,1)}, u32[]{:S(2)}) copy-start(bf16[512,512]{1,0:T(8,128)(2,1)} %param.9) | copy-start | bytes 1572868
  132.1 81.2 %all-to-all-start = ((bf16[8,512,512]{1,2,0:T(8,128)(2,1)}), bf16[8,512,512]{1,2,0:T(8,128)(2,1)}, u32[]{:S(2)}, u32[]{:S(2)}) async-start(bf16[8,512,512]{1,2,0:T(8,128)(2,1)} %stack.2), calls=%async_computation | async-start | bytes 8388608 | tf_op jit(solution)/shard_map/all_to_all | solution.py:110
  213.3 5.9 %copy-start.2 = (bf16[512,256]{1,0:T(8,128)(2,1)S(1)}, bf16[512,256]{1,0:T(8,128)(2,1)}, u32[]{:S(2)}) copy-start(bf16[512,256]{1,0:T(8,128)(2,1)} %param.12) | copy-start | bytes 786436
  213.3 5.9 %copy-start.5 = (s32[512]{0:T(512)S(1)}, s32[512]{0:T(512)}, u32[]{:S(2)}) copy-start(s32[512]{0:T(512)} %param.15) | copy-start | bytes 6148
  213.3 5.9 %copy-start.6 = (s32[512]{0:T(512)S(1)}, s32[512]{0:T(512)}, u32[]{:S(2)}) copy-start(s32[512]{0:T(512)} %param.14) | copy-start | bytes 6148
  213.3 13.1 %copy-start.3 = (f32[512]{0:T(512)S(1)}, f32[512]{0:T(512)}, u32[]{:S(2)}) copy-start(f32[512]{0:T(512)} %param.16) | copy-start | bytes 6148
  219.2 23.0 %copy-start.4 = (f32[512]{0:T(512)S(1)}, f32[512]{0:T(512)}, u32[]{:S(2)}) copy-start(f32[512]{0:T(512)} %param.17) | copy-start | bytes 6148
  220.5 13.7 %all-to-all-start.1 = ((f32[8,2,512]{2,1,0:T(2,128)}), f32[8,2,512]{2,1,0:T(2,128)S(1)}, u32[]{:S(2)}, u32[]{:S(2)}) async-start(f32[8,2,512]{2,1,0:T(2,128)} %broadcast_in_dim.4), calls=%async_computation.1 | async-start | bytes 65536 | tf_op jit(solution)/shard_map/all_to_all | solution.py:14
  235.7 15.7 %all-to-all-start.2 = ((f32[32,2,512]{2,1,0:T(2,128)}), f32[32,2,512]{2,1,0:T(2,128)S(1)}, u32[]{:S(2)}, u32[]{:S(2)}) async-start(f32[32,2,512]{2,1,0:T(2,128)} %broadcast_in_dim.5), calls=%async_computation.2 | async-start | bytes 262144 | tf_op jit(solution)/shard_map/all_to_all | solution.py:14
  253.1 10.9 %all-to-all-start.4 = ((bf16[8,64,1]{1,2,0:T(2,128)(2,1)}), bf16[8,64,1]{1,2,0:T(2,128)(2,1)S(1)}, u32[]{:S(2)}, u32[]{:S(2)}) async-start(bf16[8,64,1]{1,2,0:T(2,128)(2,1)} %convert_element_type.49), calls=%async_computation.4 | async-start | bytes 8192 | tf_op jit(solution)/shard_map/all_to_all | solution.py:76
  263.9 12.1 %all-to-all-start.3 = ((bf16[8,64,256]{2,1,0:T(8,128)(2,1)}), bf16[8,64,256]{2,1,0:T(8,128)(2,1)S(1)}, u32[]{:S(2)}, u32[]{:S(2)}) async-start(bf16[8,64,256]{2,1,0:T(8,128)(2,1)} %bitcast.10), calls=%async_computation.3 | async-start | bytes 524288 | tf_op jit(solution)/shard_map/all_to_all | solution.py:76
Sparse Core Ops, SparseCore 0:
  9.8 102.4 all-gather.2
  114.2 98.9 all-gather.4
